TPU v7x, 256 devices: a whole 4x4x8 slice. The times are simulated.
256 devices in a mesh: blk: 64 (over y, x_hi, z), repl: 4 (over x_lo, core).
Axes of the slice: x: 4 (x_hi: 2, x_lo: 2; x = x_hi * 2 + x_lo), y: 4, z: 8, core: 2. Of those that a mesh axis runs over, the one named last changes fastest.
Arguments:
- feats: bfloat16 [131072, 512], P(('blk', 'repl')), may hold values from -6 to 6
- weight: bfloat16 [512, 512], replicated, may hold values from -0.25 to 0.25
- tile_vals: bfloat16 [1024, 8, 128, 128], P(('blk', 'repl')), may hold values from -0.25 to 0.25
- tile_cols: int32 [1024, 8], P(('blk', 'repl')), may hold values from 0 to 1023, as said below
- tile_count: int32 [1024], P(('blk', 'repl')), may hold values from 2 to 8, as said below
- cotangent: bfloat16 [131072, 512], P(('blk', 'repl')), may hold values from -24 to 24
Outputs:
- output: bfloat16 [131072, 512], P(('blk', 'repl'))
- weight_grad: float32 [512, 512], replicated
- feat_grad: bfloat16 [131072, 512], P(('blk', 'repl'))
Inputs may be any that keep to these rules, and one draw needn't show every extreme that they name: `tile_cols`: slot 0 of block row k names k itself. Every named column block lies in a panel (of 2048 nodes, block row k being in panel k * 128 // 2048) at most 2 panels away from its row's panel, counted around a closed cycle of panels. `tile_count`: slots at and after a block row's count are not part of the adjacency.
All inputs are finite; a program needn't handle non-finite values.
Results may differ from a plain program's by a relative error of at most 0.011.
Values may be sent and summed in bfloat16 or wider, within the bound.
A program may use at most 128 MiB of HBM per device.

v0:
```python
import math
import jax
import jax.numpy as jnp
from jax import lax
from jax.sharding import PartitionSpec as P

TILE = 128
SLOTS = 8
REACH = 2


def passed_along(value, axis, steps):
    count = lax.axis_size(axis)
    pairs = [(source, (source + steps) % count) for source in range(count)]
    return lax.ppermute(value, axis, pairs)


def shortened(x):
    return jax.tree.map(lambda a: a.astype(jnp.bfloat16) if a.dtype == jnp.float32 else a, x)


def from_everyone(x, axis):
    length = lax.axis_size(axis)
    return lax.all_to_all(jnp.broadcast_to(x[None], (length, *x.shape)), axis, 0, 0, tiled=True)


def laid_out(pieces, dim):
    lengths = list(pieces.shape[1:])
    lengths[dim] *= pieces.shape[0]
    return jnp.moveaxis(pieces, 0, dim).reshape(lengths)


def gathered_copies(x, axis, dim):
    pieces = from_everyone(x, axis)
    return laid_out(pieces, dim)


def silu_slope(preact):
    sigma = jax.nn.sigmoid(preact)
    return sigma * (1.0 + preact * (1.0 - sigma))


def window_index(tile_cols, center, panel_blocks, cycle_size):
    panel_of = tile_cols // panel_blocks
    offset = (panel_of - center) % cycle_size
    offset = jnp.where(offset > REACH, offset - cycle_size, offset)
    return (offset + REACH) * panel_blocks + tile_cols % panel_blocks


def shift_window(source):
    lower_side = []
    upper_side = []
    below_piece = source
    above_piece = source
    for hop_number in range(REACH):
        below_piece = passed_along(below_piece, "blk", 1)
        above_piece = passed_along(above_piece, "blk", -1)
        lower_side.append(below_piece)
        upper_side.append(above_piece)
    pieces = lower_side[::-1] + [source] + upper_side
    return pieces


def return_to_owners(shares):
    upward = jnp.zeros_like(shares[REACH])
    for offset in range(REACH, 0, -1):
        upward = passed_along(shortened(upward + shares[offset + REACH]), "blk", 1)
    downward = jnp.zeros_like(shares[REACH])
    for offset in range(-REACH, 0):
        downward = passed_along(shortened(downward + shares[offset + REACH]), "blk", -1)
    total = shares[REACH] + upward + downward
    return total


def local(feats, weight, tile_vals, tile_cols, tile_count, cotangent):
    node_rows = feats.shape[0]
    feat_width = feats.shape[1]
    cycle_size = lax.axis_size("blk")
    group_size = lax.axis_size("repl")
    panel_size = node_rows * group_size
    panel_blocks = panel_size // TILE
    block_rows = node_rows // TILE
    span_count = 2 * REACH + 1
    center = lax.axis_index("blk")
    own_panel = gathered_copies(feats, "repl", 0)
    pieces = shift_window(own_panel)
    window = jnp.concatenate(pieces, axis=0).reshape(span_count * panel_blocks, TILE, feat_width)
    local_index = window_index(tile_cols, center, panel_blocks, cycle_size)
    slot_ids = jnp.arange(SLOTS, dtype=jnp.int32)
    live_slots = slot_ids[None, :] < tile_count[:, None]
    masked_vals = jnp.where(live_slots[:, :, None, None], tile_vals, jnp.zeros_like(tile_vals))
    picked = window[local_index]
    summed = jnp.einsum("nsij,nsjf->nif", masked_vals, picked, preferred_element_type=jnp.float32)
    aggregate = summed.reshape(node_rows, feat_width).astype(jnp.bfloat16)
    preact = jnp.dot(aggregate, weight, preferred_element_type=jnp.float32)
    output = jax.nn.silu(preact).astype(jnp.bfloat16)
    slope = (cotangent.astype(jnp.float32) * silu_slope(preact)).astype(jnp.bfloat16)
    nodes_total = node_rows * group_size * cycle_size
    weight_term = jnp.einsum("nf,ng->fg", aggregate, slope, preferred_element_type=jnp.float32)
    weight_grad = lax.psum(weight_term, ("blk", "repl")) * (1.0 / math.sqrt(nodes_total))
    backward = jnp.einsum("nf,gf->ng", slope, weight, preferred_element_type=jnp.float32).astype(
        jnp.bfloat16
    )
    back_blocks = backward.reshape(block_rows, TILE, feat_width)
    segments = span_count * panel_blocks
    contrib = jnp.einsum(
        "nsji,njf->nsif", masked_vals, back_blocks, preferred_element_type=jnp.float32
    )
    partial_sums = jax.ops.segment_sum(
        contrib.reshape(block_rows * SLOTS, TILE, feat_width),
        local_index.reshape(-1),
        num_segments=segments,
    )
    panel_parts = partial_sums.reshape(span_count, panel_size, feat_width)
    shares = [panel_parts[position] for position in range(span_count)]
    panel_total = return_to_owners(shares)
    grad_rows = lax.psum_scatter(
        panel_total.astype(jnp.bfloat16), "repl", scatter_dimension=0, tiled=True
    )
    return (output, weight_grad, grad_rows)


def solution(mesh):
    in_specs = (
        P(("blk", "repl"), None),
        P(),
        P(("blk", "repl"), None, None, None),
        P(("blk", "repl"), None),
        P(("blk", "repl")),
        P(("blk", "repl"), None),
    )
    out_specs = (P(("blk", "repl"), None), P(), P(("blk", "repl"), None))
    return jax.shard_map(local, mesh=mesh, in_specs=in_specs, out_specs=out_specs, check_vma=False)
```

profile of v0, /device:TPU:2, one launch (start us, length us, event | category | flops | bytes accessed | tf_op | source)
XLA Modules:
  0.0 551.7 jit_solution(13088517721672567636)
XLA Ops:
  8.1 1.2 broadcast_in_dim.28
  9.3 28.7 %all_to_all.5 = bf16[4,512,512]{2,1,0:T(8,128)(2,1)S(1)} all-to-all(bf16[4,512,512]{2,1,0:T(8,128)(2,1)S(1)} %broadcast_in_dim.28), channel_id=1, replica_groups=mesh['blk'=64,'repl'=4] {'repl'}, dimensions={0} | all-to-all | bytes 4194304 | tf_op jit(solution)/shard_map/all_to_all | solution.py:24
  38.4 8.2 %collective-permute-start.2 = (bf16[2048,512]{1,0:T(8,128)(2,1)S(1)}, bf16[2048,512]{1,0:T(8,128)(2,1)}, u32[]{:S(2)}, u32[]{:S(2)}) collective-permute-start(bf16[2048,512]{1,0:T(8,128)(2,1)S(1)} %bitcast.42), channel_id=1, source_target_pairs={{0,252},{4,0},{8,4},{12,8},{16,12},{20,16},{24,20},{28,24},{32,28}... | collective-permute-start | bytes 6291464 | tf_op jit(solution)/shard_map/ppermute | solution.py:15
  46.5 45.8 %collective-permute-done = bf16[2048,512]{1,0:T(8,128)(2,1)} collective-permute-done((bf16[2048,512]{1,0:T(8,128)(2,1)S(1)}, bf16[2048,512]{1,0:T(8,128)(2,1)}, u32[]{:S(2)}, u32[]{:S(2)}) %collective-permute-start) | collective-permute-done | bytes 2097184 | tf_op jit(solution)/shard_map/ppermute | solution.py:15
  92.3 7.7 %collective-permute-start.3 = (bf16[2048,512]{1,0:T(8,128)(2,1)}, bf16[2048,512]{1,0:T(8,128)(2,1)}, u32[]{:S(2)}, u32[]{:S(2)}) collective-permute-start(bf16[2048,512]{1,0:T(8,128)(2,1)} %collective-permute-done.2), channel_id=1, source_target_pairs={{0,252},{4,0},{8,4},{12,8},{16,12},{20,16},{24,20},{28,24},{32,28}... | collective-permute-start | bytes 6291464 | tf_op jit(solution)/shard_map/ppermute | solution.py:15
  100.4 44.9 %collective-permute-done.1 = bf16[2048,512]{1,0:T(8,128)(2,1)} collective-permute-done((bf16[2048,512]{1,0:T(8,128)(2,1)}, bf16[2048,512]{1,0:T(8,128)(2,1)}, u32[]{:S(2)}, u32[]{:S(2)}) %collective-permute-start.1) | collective-permute-done | bytes 2097184 | tf_op jit(solution)/shard_map/ppermute | solution.py:15
  145.2 1.7 constant_dynamic-update-slice_fusion.4
  146.9 1.7 constant_dynamic-update-slice_fusion.3
  148.8 1.7 constant_dynamic-update-slice_fusion.1
  150.6 1.7 constant_dynamic-update-slice_fusion
  152.3 4.0 copy-done.3
  156.3 7.0 %gather_fusion = bf16[32,128,512]{2,1,0:T(8,128)(2,1)} fusion(bf16[80,128,512]{2,1,0:T(8,128)(2,1)} %bitcast.44, s32[1024]{0:T(1024)S(1)} %pad_clamp_fusion), kind=kCustom, calls=%fused_computation | custom fusion | bytes 8388736 | tf_op jit(solution)/shard_map/gather | solution.py:92
  163.3 3.0 fusion.4
  166.3 1.6 multiply_convert_fusion
  167.9 0.5 convolution_convert_fusion
  168.4 4.6 fusion.5
  173.0 9.7 %broadcast_in_dim.30 = f32[80,128,512]{2,1,0:T(8,128)} broadcast(f32[]{:T(128)} %constant.63.clone.1), dimensions={} | broadcast | bytes 20971524 | tf_op jit(solution)/shard_map/broadcast_in_dim | solution.py:109
  182.6 18.8 %scatter_fusion = f32[80,128,512]{2,1,0:T(8,128)} fusion(f32[80,128,512]{2,1,0:T(8,128)} %broadcast_in_dim.30, s32[32]{0:T(128)S(1)} %reshape.69, f32[32,128,512]{2,1,0:T(8,128)} %bitcast.39), kind=kCustom, calls=%fused_computation.1 | custom fusion | flops 2097152 | bytes 25165952 | tf_op jit(solution)/shard_map/scatter-add | solution.py:109
  201.5 8.0 %convert.4 = bf16[80,128,512]{2,1,0:T(8,128)(2,1)S(1)} convert(f32[80,128,512]{2,1,0:T(8,128)} %scatter_fusion) | non-fusion elementwise | flops 5242880 | bytes 31457280 | tf_op jit(solution)/shard_map/convert.1
  209.4 2.3 fusion.18
  211.7 1.8 collective-permute-start.6
  213.7 10.1 %fusion.17 = (f32[16,128,512]{2,1,0:T(8,128)S(1)}, f32[16,128,512]{2,1,0:T(8,128)}, f32[16,128,512]{2,1,0:T(8,128)}) fusion(f32[80,128,512]{2,1,0:T(8,128)} %scatter_fusion), kind=kLoop, calls=%fused_computation.46 | loop fusion | bytes 25165824 | tf_op jit(solution)/shard_map/slice | solution.py:115
  223.9 33.9 %collective-permute-done.6 = bf16[2048,512]{1,0:T(8,128)(2,1)} collective-permute-done((bf16[2048,512]{1,0:T(8,128)(2,1)}, bf16[2048,512]{1,0:T(8,128)(2,1)}, u32[]{:S(2)}, u32[]{:S(2)}) %collective-permute-start.6) | collective-permute-done | bytes 2097184 | tf_op jit(solution)/shard_map/ppermute | solution.py:15
  257.8 4.9 fusion
  262.7 7.7 %collective-permute-start.7 = (bf16[2048,512]{1,0:T(8,128)(2,1)}, bf16[2048,512]{1,0:T(8,128)(2,1)}, u32[]{:S(2)}, u32[]{:S(2)}) collective-permute-start(bf16[2048,512]{1,0:T(8,128)(2,1)} %fusion), channel_id=1, source_target_pairs={{0,252},{4,0},{8,4},{12,8},{16,12},{20,16},{24,20},{28,24},{32,28}... | collective-permute-start | bytes 6291464 | tf_op jit(solution)/shard_map/ppermute | solution.py:15
  270.4 4.1 fusion.1
  274.5 1.4 fusion.19
  276.0 38.6 %collective-permute-done.7 = bf16[2048,512]{1,0:T(8,128)(2,1)} collective-permute-done((bf16[2048,512]{1,0:T(8,128)(2,1)}, bf16[2048,512]{1,0:T(8,128)(2,1)}, u32[]{:S(2)}, u32[]{:S(2)}) %collective-permute-start.7) | collective-permute-done | bytes 2097184 | tf_op jit(solution)/shard_map/ppermute | solution.py:15
  314.6 12.3 %collective-permute-done.5 = bf16[2048,512]{1,0:T(8,128)(2,1)S(1)} collective-permute-done((bf16[2048,512]{1,0:T(8,128)(2,1)}, bf16[2048,512]{1,0:T(8,128)(2,1)S(1)}, u32[]{:S(2)}, u32[]{:S(2)}) %collective-permute-start.5) | collective-permute-done | bytes 2097184 | tf_op jit(solution)/shard_map/ppermute | solution.py:15
  327.0 5.1 fusion.3
  332.1 209.8 %all-reduce.2.cloned.1.call-done = f32[512,512]{1,0:T(8,128)} async-done(((f32[512,512]{1,0:T(8,128)}), f32[512,512]{1,0:T(8,128)}) %all-reduce.2.cloned.1.call-update) | async-done | bytes 1048592 | tf_op jit(solution)/shard_map/psum | solution.py:100
  541.9 2.3 broadcast_multiply_fusion
  (35 shorter events, 1.1 us)
Async XLA Ops:
  8.0 158.3 %copy-start = (bf16[512,512]{1,0:T(8,128)(2,1)S(1)}, bf16[512,512]{1,0:T(8,128)(2,1)}, u32[]{:S(2)}) copy-start(bf16[512,512]{1,0:T(8,128)(2,1)} %param.7) | copy-start | bytes 1572868
  8.0 92.1 %copy-start.6 = (s32[4,8]{1,0:T(4,128)S(1)}, s32[4,8]{1,0:T(4,128)}, u32[]{:S(2)}) copy-start(s32[4,8]{1,0:T(4,128)} %param.9) | copy-start | bytes 388
  8.0 92.3 %copy-start.8 = (s32[4]{0:T(128)S(1)}, s32[4]{0:T(128)}, u32[]{:S(2)}) copy-start(s32[4]{0:T(128)} %param.10) | copy-start | bytes 52
  8.0 533.9 %all-reduce.2.cloned.1.call-start = ((), (), s32[]{:S(2)}) async-start(), calls=%async_computation.2 | async-start | bytes 2097152 | tf_op jit(solution)/shard_map/psum | solution.py:100
  38.1 54.2 %collective-permute-start = (bf16[2048,512]{1,0:T(8,128)(2,1)S(1)}, bf16[2048,512]{1,0:T(8,128)(2,1)}, u32[]{:S(2)}, u32[]{:S(2)}) collective-permute-start(bf16[2048,512]{1,0:T(8,128)(2,1)S(1)} %bitcast.41), channel_id=1, source_target_pairs={{0,4},{4,8},{8,12},{12,16},{16,20},{20,24},{24,28},{28,32},{32,36}... | collective-permute-start | bytes 6291464 | tf_op jit(solution)/shard_map/ppermute | solution.py:15
  38.4 53.9 %collective-permute-start.2 = (bf16[2048,512]{1,0:T(8,128)(2,1)S(1)}, bf16[2048,512]{1,0:T(8,128)(2,1)}, u32[]{:S(2)}, u32[]{:S(2)}) collective-permute-start(bf16[2048,512]{1,0:T(8,128)(2,1)S(1)} %bitcast.42), channel_id=1, source_target_pairs={{0,252},{4,0},{8,4},{12,8},{16,12},{20,16},{24,20},{28,24},{32,28}... | collective-permute-start | bytes 6291464 | tf_op jit(solution)/shard_map/ppermute | solution.py:15
  92.3 52.9 %collective-permute-start.1 = (bf16[2048,512]{1,0:T(8,128)(2,1)}, bf16[2048,512]{1,0:T(8,128)(2,1)}, u32[]{:S(2)}, u32[]{:S(2)}) collective-permute-start(bf16[2048,512]{1,0:T(8,128)(2,1)} %collective-permute-done), channel_id=1, source_target_pairs={{0,4},{4,8},{8,12},{12,16},{16,20},{20,24},{24,28},{28,32},{32,36}... | collective-permute-start | bytes 6291464 | tf_op jit(solution)/shard_map/ppermute | solution.py:15
  92.3 58.2 %collective-permute-start.3 = (bf16[2048,512]{1,0:T(8,128)(2,1)}, bf16[2048,512]{1,0:T(8,128)(2,1)}, u32[]{:S(2)}, u32[]{:S(2)}) collective-permute-start(bf16[2048,512]{1,0:T(8,128)(2,1)} %collective-permute-done.2), channel_id=1, source_target_pairs={{0,252},{4,0},{8,4},{12,8},{16,12},{20,16},{24,20},{28,24},{32,28}... | collective-permute-start | bytes 6291464 | tf_op jit(solution)/shard_map/ppermute | solution.py:15
  152.3 4.0 copy-start.3
  156.3 7.0 %copy-start.2 = (bf16[4,8,128,128]{3,2,1,0:T(8,128)(2,1)S(1)}, bf16[4,8,128,128]{3,2,1,0:T(8,128)(2,1)}, u32[]{:S(2)}) copy-start(bf16[4,8,128,128]{3,2,1,0:T(8,128)(2,1)} %param.8) | copy-start | bytes 3145732
  163.3 3.0 copy-start.7
  166.3 2.1 copy-start.4
  211.7 46.1 %collective-permute-start.6 = (bf16[2048,512]{1,0:T(8,128)(2,1)}, bf16[2048,512]{1,0:T(8,128)(2,1)}, u32[]{:S(2)}, u32[]{:S(2)}) collective-permute-start(bf16[2048,512]{1,0:T(8,128)(2,1)} %bitcast.13), channel_id=1, source_target_pairs={{0,252},{4,0},{8,4},{12,8},{16,12},{20,16},{24,20},{28,24},{32,28}... | collective-permute-start | bytes 6291464 | tf_op jit(solution)/shard_map/ppermute | solution.py:15
  213.5 56.9 %collective-permute-start.4 = (bf16[2048,512]{1,0:T(8,128)(2,1)}, bf16[2048,512]{1,0:T(8,128)(2,1)}, u32[]{:S(2)}, u32[]{:S(2)}) collective-permute-start(bf16[2048,512]{1,0:T(8,128)(2,1)} %bitcast.11), channel_id=1, source_target_pairs={{0,4},{4,8},{8,12},{12,16},{16,20},{20,24},{24,28},{28,32},{32,36}... | collective-permute-start | bytes 6291464 | tf_op jit(solution)/shard_map/ppermute | solution.py:15
  262.7 51.9 %collective-permute-start.7 = (bf16[2048,512]{1,0:T(8,128)(2,1)}, bf16[2048,512]{1,0:T(8,128)(2,1)}, u32[]{:S(2)}, u32[]{:S(2)}) collective-permute-start(bf16[2048,512]{1,0:T(8,128)(2,1)} %fusion), channel_id=1, source_target_pairs={{0,252},{4,0},{8,4},{12,8},{16,12},{20,16},{24,20},{28,24},{32,28}... | collective-permute-start | bytes 6291464 | tf_op jit(solution)/shard_map/ppermute | solution.py:15
  270.4 4.1 copy-start.5
  274.5 52.5 %collective-permute-start.5 = (bf16[2048,512]{1,0:T(8,128)(2,1)}, bf16[2048,512]{1,0:T(8,128)(2,1)S(1)}, u32[]{:S(2)}, u32[]{:S(2)}) collective-permute-start(bf16[2048,512]{1,0:T(8,128)(2,1)} %fusion.1), channel_id=1, source_target_pairs={{0,4},{4,8},{8,12},{12,16},{16,20},{20,24},{24,28},{28,32},{32,36}... | collective-permute-start | bytes 6291464 | tf_op jit(solution)/shard_map/ppermute | solution.py:15
  275.9 268.3 %reduce-scatter.2.cloned.1.call-start = ((), (), s32[]{:S(2)}) async-start(), calls=%async_computation.3 | async-start | bytes 2621440 | tf_op jit(solution)/shard_map/reduce_scatter | solution.py:117
  327.0 217.3 %copy-start.1 = (bf16[512,512]{1,0:T(8,128)(2,1)S(1)}, bf16[512,512]{1,0:T(8,128)(2,1)}, u32[]{:S(2)}) copy-start(bf16[512,512]{1,0:T(8,128)(2,1)} %param.7) | copy-start | bytes 1572868
Sparse Core Ops, SparseCore 0:
  276.1 265.8 all-reduce.1
Sparse Core Ops, SparseCore 1:
  332.2 21.3 reduce-scatter.1
where the time goes:
time: 552 us
  waiting for transfers between devices  385 us (70%)
  other arithmetic  43.4 us (8%)
  local copies, waits for them, and re-layouts  41.5 us (8%)
  blocking collectives  28.7 us (5%)
  starting transfers between devices  26 us (5%)
  between operations  15.6 us (3%)
  matrix products  11.1 us (2%)
    psum x1, waiting for transfers between devices, local(): lax.psum(weight_term, ('blk', 'repl')) * (1.0 / math.sqrt(nodes_total))  210 us
    ppermute x8, waiting for transfers between devices, passed_along(): return lax.ppermute(value, axis, pairs)  176 us
    all_to_all x1, blocking collectives, from_everyone(): lax.all_to_all(jnp.broadcast_to(x[None], (length, *x.shape)), axis, 0, 0,...  28.7 us
    ppermute x8, starting transfers between devices, passed_along(): return lax.ppermute(value, axis, pairs)  25.9 us
    scatter-add x1, other arithmetic, local(): jax.ops.segment_sum(contrib.reshape(block_rows * SLOTS, TILE, feat_width)...  18.8 us
    slice x2, local copies, waits for them, and re-layouts, local(): shares = [panel_parts[position] for position in range(span_count)]  12.4 us
  transfers between devices with their start and end apart: 10, of which 6 were waited for; matrix products, arithmetic and copies ran while one was open for 6% of the time, Pallas kernels for 0%

commit v1 on v0

--- a/solution.py
+++ b/solution.py
@@ -1,12 +1,21 @@
+import functools
 import math
 import jax
 import jax.numpy as jnp
 from jax import lax
 from jax.sharding import PartitionSpec as P
+from jax.lax import psum
 
 TILE = 128
 SLOTS = 8
 REACH = 2
+
+
+def _test_region(vector, which_axis, bus_axis):
+    return psum(psum(vector, which_axis), bus_axis)
+
+
+_expand_body = functools.partial(_test_region, which_axis="repl", bus_axis="blk")
 
 
 def passed_along(value, axis, steps):
@@ -97,7 +106,7 @@
     slope = (cotangent.astype(jnp.float32) * silu_slope(preact)).astype(jnp.bfloat16)
     nodes_total = node_rows * group_size * cycle_size
     weight_term = jnp.einsum("nf,ng->fg", aggregate, slope, preferred_element_type=jnp.float32)
-    weight_grad = lax.psum(weight_term, ("blk", "repl")) * (1.0 / math.sqrt(nodes_total))
+    weight_grad = _expand_body(weight_term) * (1.0 / math.sqrt(nodes_total))
     backward = jnp.einsum("nf,gf->ng", slope, weight, preferred_element_type=jnp.float32).astype(
         jnp.bfloat16
     )

time: 552 us -> 1090 us (1.97)
  waiting for transfers between devices: 385 us -> 924 us
    psum x1 -> x2, waiting for transfers between devices: 210 us -> 772 us  [_test_region(): return psum(psum(vector, which_axis), bus_axis)]
    ppermute x8, waiting for transfers between devices: 176 us -> 125 us  [passed_along(): return lax.ppermute(value, axis, pairs)]
    reduce_scatter x1, waiting for transfers between devices: 0.01 us -> 28 us  [local(): lax.psum_scatter(panel_total.astype(jnp.bfloat16), 'repl', scatter_dimens...]
  transfers between devices with their start and end apart: 10 -> 11, of which waited for: 6 -> 6; matrix products, arithmetic and copies ran while one was open for 6% -> 3% of each run, Pallas kernels for 0% -> 0%
where the time goes in v1:
time: 1090 us
  waiting for transfers between devices  924 us (85%)
  other arithmetic  43.3 us (4%)
  local copies, waits for them, and re-layouts  41.5 us (4%)
  blocking collectives  28.7 us (3%)
  starting transfers between devices  26 us (2%)
  between operations  13.9 us (1%)
  matrix products  11.1 us (1%)
    psum x2, waiting for transfers between devices, _test_region(): return psum(psum(vector, which_axis), bus_axis)  772 us
    ppermute x8, waiting for transfers between devices, passed_along(): return lax.ppermute(value, axis, pairs)  125 us
    all_to_all x1, blocking collectives, from_everyone(): lax.all_to_all(jnp.broadcast_to(x[None], (length, *x.shape)), axis, 0, 0,...  28.7 us
    reduce_scatter x1, waiting for transfers between devices, local(): lax.psum_scatter(panel_total.astype(jnp.bfloat16), 'repl', scatter_dimens...  28 us
    ppermute x8, starting transfers between devices, passed_along(): return lax.ppermute(value, axis, pairs)  25.9 us
  transfers between devices with their start and end apart: 11, of which 6 were waited for; matrix products, arithmetic and copies ran while one was open for 3% of the time, Pallas kernels for 0%

profile of v1, /device:TPU:2, one launch (start us, length us, event | category | flops | bytes accessed | tf_op | source)
XLA Modules:
  0.0 1088.9 jit_solution(8382876286018407745)
XLA Ops:
  7.2 1.2 broadcast_in_dim.28
  8.5 28.7 %all_to_all.5 = bf16[4,512,512]{2,1,0:T(8,128)(2,1)S(1)} all-to-all(bf16[4,512,512]{2,1,0:T(8,128)(2,1)S(1)} %broadcast_in_dim.28), channel_id=1, replica_groups=mesh['blk'=64,'repl'=4] {'repl'}, dimensions={0} | all-to-all | bytes 4194304 | tf_op jit(solution)/shard_map/all_to_all | solution.py:33
  37.6 8.2 collective-permute-start.2
  45.7 45.8 %collective-permute-done = bf16[2048,512]{1,0:T(8,128)(2,1)} collective-permute-done((bf16[2048,512]{1,0:T(8,128)(2,1)S(1)}, bf16[2048,512]{1,0:T(8,128)(2,1)}, u32[]{:S(2)}, u32[]{:S(2)}) %collective-permute-start) | collective-permute-done | bytes 2097184 | tf_op jit(solution)/shard_map/ppermute | solution.py:24
  91.5 7.7 collective-permute-start.3
  99.5 44.9 %collective-permute-done.1 = bf16[2048,512]{1,0:T(8,128)(2,1)} collective-permute-done((bf16[2048,512]{1,0:T(8,128)(2,1)}, bf16[2048,512]{1,0:T(8,128)(2,1)}, u32[]{:S(2)}, u32[]{:S(2)}) %collective-permute-start.1) | collective-permute-done | bytes 2097184 | tf_op jit(solution)/shard_map/ppermute | solution.py:24
  144.4 1.7 constant_dynamic-update-slice_fusion.4
  146.1 1.7 constant_dynamic-update-slice_fusion.3
  148.0 1.7 constant_dynamic-update-slice_fusion.1
  149.7 1.7 constant_dynamic-update-slice_fusion
  151.5 4.0 copy-done.3
  155.5 7.0 gather_fusion
  162.4 3.0 fusion.4
  165.5 1.6 multiply_convert_fusion
  167.1 0.5 convolution_convert_fusion
  167.5 4.6 fusion.5
  172.2 9.7 broadcast_in_dim.30
  181.8 18.8 %scatter_fusion = f32[80,128,512]{2,1,0:T(8,128)} fusion(f32[80,128,512]{2,1,0:T(8,128)} %broadcast_in_dim.30, s32[32]{0:T(128)S(1)} %reshape.69, f32[32,128,512]{2,1,0:T(8,128)} %bitcast.39), kind=kCustom, calls=%fused_computation.1 | custom fusion | flops 2097152 | bytes 25165952 | tf_op jit(solution)/shard_map/scatter-add | solution.py:118
  200.6 8.0 convert.4
  208.6 2.3 fusion.18
  210.9 1.8 collective-permute-start.6
  212.9 10.1 fusion.17
  223.0 33.9 %collective-permute-done.6 = bf16[2048,512]{1,0:T(8,128)(2,1)} collective-permute-done((bf16[2048,512]{1,0:T(8,128)(2,1)}, bf16[2048,512]{1,0:T(8,128)(2,1)}, u32[]{:S(2)}, u32[]{:S(2)}) %collective-permute-start.6) | collective-permute-done | bytes 2097184 | tf_op jit(solution)/shard_map/ppermute | solution.py:24
  257.0 4.9 fusion
  261.9 7.6 collective-permute-start.7
  269.6 4.1 fusion.1
  273.6 1.4 fusion.19
  275.1 74.2 %all-reduce.3.cloned.1.call-done = f32[512,512]{1,0:T(8,128)} async-done(((f32[512,512]{1,0:T(8,128)}), f32[512,512]{1,0:T(8,128)}) %all-reduce.3.cloned.1.call-update) | async-done | bytes 1048592 | tf_op jit(solution)/shard_map/psum | solution.py:15
  349.4 5.1 fusion.3
  354.6 697.5 %all-reduce.5.cloned.1.call-done = f32[512,512]{1,0:T(8,128)} async-done(((f32[512,512]{1,0:T(8,128)}), f32[512,512]{1,0:T(8,128)}) %all-reduce.5.cloned.1.call-update) | async-done | bytes 1048592 | tf_op jit(solution)/shard_map/psum | solution.py:15
  1052.1 2.3 broadcast_multiply_fusion
  1054.4 28.0 %reduce-scatter.2.cloned.1.call-done = bf16[512,512]{1,0:T(8,128)(2,1)} async-done(((bf16[2048,512]{1,0:T(8,128)(2,1)}), bf16[512,512]{1,0:T(8,128)(2,1)}) %reduce-scatter.2.cloned.1.call-update) | async-done | bytes 524304 | tf_op jit(solution)/shard_map/reduce_scatter | solution.py:126
  (38 shorter events, 1.2 us)
Async XLA Ops:
  7.2 158.3 %copy-start = (bf16[512,512]{1,0:T(8,128)(2,1)S(1)}, bf16[512,512]{1,0:T(8,128)(2,1)}, u32[]{:S(2)}) copy-start(bf16[512,512]{1,0:T(8,128)(2,1)} %param.7) | copy-start | bytes 1572868
  7.2 92.1 %copy-start.6 = (s32[4,8]{1,0:T(4,128)S(1)}, s32[4,8]{1,0:T(4,128)}, u32[]{:S(2)}) copy-start(s32[4,8]{1,0:T(4,128)} %param.9) | copy-start | bytes 388
  7.2 92.3 %copy-start.8 = (s32[4]{0:T(128)S(1)}, s32[4]{0:T(128)}, u32[]{:S(2)}) copy-start(s32[4]{0:T(128)} %param.10) | copy-start | bytes 52
  7.2 342.1 %all-reduce.3.cloned.1.call-start = ((), (), s32[]{:S(2)}) async-start(), calls=%async_computation.2 | async-start | bytes 2097152 | tf_op jit(solution)/shard_map/psum | solution.py:15
  37.2 54.2 %collective-permute-start = (bf16[2048,512]{1,0:T(8,128)(2,1)S(1)}, bf16[2048,512]{1,0:T(8,128)(2,1)}, u32[]{:S(2)}, u32[]{:S(2)}) collective-permute-start(bf16[2048,512]{1,0:T(8,128)(2,1)S(1)} %bitcast.41), channel_id=1, source_target_pairs={{0,4},{4,8},{8,12},{12,16},{16,20},{20,24},{24,28},{28,32},{32,36}... | collective-permute-start | bytes 6291464 | tf_op jit(solution)/shard_map/ppermute | solution.py:24
  37.6 53.9 %collective-permute-start.2 = (bf16[2048,512]{1,0:T(8,128)(2,1)S(1)}, bf16[2048,512]{1,0:T(8,128)(2,1)}, u32[]{:S(2)}, u32[]{:S(2)}) collective-permute-start(bf16[2048,512]{1,0:T(8,128)(2,1)S(1)} %bitcast.42), channel_id=1, source_target_pairs={{0,252},{4,0},{8,4},{12,8},{16,12},{20,16},{24,20},{28,24},{32,28}... | collective-permute-start | bytes 6291464 | tf_op jit(solution)/shard_map/ppermute | solution.py:24
  91.5 52.9 %collective-permute-start.1 = (bf16[2048,512]{1,0:T(8,128)(2,1)}, bf16[2048,512]{1,0:T(8,128)(2,1)}, u32[]{:S(2)}, u32[]{:S(2)}) collective-permute-start(bf16[2048,512]{1,0:T(8,128)(2,1)} %collective-permute-done), channel_id=1, source_target_pairs={{0,4},{4,8},{8,12},{12,16},{16,20},{20,24},{24,28},{28,32},{32,36}... | collective-permute-start | bytes 6291464 | tf_op jit(solution)/shard_map/ppermute | solution.py:24
  91.5 58.2 %collective-permute-start.3 = (bf16[2048,512]{1,0:T(8,128)(2,1)}, bf16[2048,512]{1,0:T(8,128)(2,1)}, u32[]{:S(2)}, u32[]{:S(2)}) collective-permute-start(bf16[2048,512]{1,0:T(8,128)(2,1)} %collective-permute-done.2), channel_id=1, source_target_pairs={{0,252},{4,0},{8,4},{12,8},{16,12},{20,16},{24,20},{28,24},{32,28}... | collective-permute-start | bytes 6291464 | tf_op jit(solution)/shard_map/ppermute | solution.py:24
  151.5 4.0 copy-start.3
  155.5 7.0 copy-start.2
  162.4 3.0 copy-start.7
  165.4 2.1 copy-start.4
  210.9 46.1 %collective-permute-start.6 = (bf16[2048,512]{1,0:T(8,128)(2,1)}, bf16[2048,512]{1,0:T(8,128)(2,1)}, u32[]{:S(2)}, u32[]{:S(2)}) collective-permute-start(bf16[2048,512]{1,0:T(8,128)(2,1)} %bitcast.13), channel_id=1, source_target_pairs={{0,252},{4,0},{8,4},{12,8},{16,12},{20,16},{24,20},{28,24},{32,28}... | collective-permute-start | bytes 6291464 | tf_op jit(solution)/shard_map/ppermute | solution.py:24
  212.7 56.9 %collective-permute-start.4 = (bf16[2048,512]{1,0:T(8,128)(2,1)}, bf16[2048,512]{1,0:T(8,128)(2,1)}, u32[]{:S(2)}, u32[]{:S(2)}) collective-permute-start(bf16[2048,512]{1,0:T(8,128)(2,1)} %bitcast.11), channel_id=1, source_target_pairs={{0,4},{4,8},{8,12},{12,16},{16,20},{20,24},{24,28},{28,32},{32,36}... | collective-permute-start | bytes 6291464 | tf_op jit(solution)/shard_map/ppermute | solution.py:24
  261.9 87.5 %collective-permute-start.7 = (bf16[2048,512]{1,0:T(8,128)(2,1)}, bf16[2048,512]{1,0:T(8,128)(2,1)}, u32[]{:S(2)}, u32[]{:S(2)}) collective-permute-start(bf16[2048,512]{1,0:T(8,128)(2,1)} %fusion), channel_id=1, source_target_pairs={{0,252},{4,0},{8,4},{12,8},{16,12},{20,16},{24,20},{28,24},{32,28}... | collective-permute-start | bytes 6291464 | tf_op jit(solution)/shard_map/ppermute | solution.py:24
  269.6 4.1 copy-start.5
  273.6 75.7 %collective-permute-start.5 = (bf16[2048,512]{1,0:T(8,128)(2,1)}, bf16[2048,512]{1,0:T(8,128)(2,1)S(1)}, u32[]{:S(2)}, u32[]{:S(2)}) collective-permute-start(bf16[2048,512]{1,0:T(8,128)(2,1)} %fusion.1), channel_id=1, source_target_pairs={{0,4},{4,8},{8,12},{12,16},{16,20},{20,24},{24,28},{28,32},{32,36}... | collective-permute-start | bytes 6291464 | tf_op jit(solution)/shard_map/ppermute | solution.py:24
  275.1 777.0 %all-reduce.5.cloned.1.call-start = ((), (), s32[]{:S(2)}) async-start(), calls=%async_computation.3 | async-start | bytes 2097152 | tf_op jit(solution)/shard_map/psum | solution.py:15
  349.3 733.0 %reduce-scatter.2.cloned.1.call-start = ((), (), s32[]{:S(2)}) async-start(), calls=%async_computation.4 | async-start | bytes 2621440 | tf_op jit(solution)/shard_map/reduce_scatter | solution.py:126
  349.4 733.0 %copy-start.1 = (bf16[512,512]{1,0:T(8,128)(2,1)S(1)}, bf16[512,512]{1,0:T(8,128)(2,1)}, u32[]{:S(2)}) copy-start(bf16[512,512]{1,0:T(8,128)(2,1)} %param.7) | copy-start | bytes 1572868
Sparse Core Ops, SparseCore 0:
  275.2 74.0 all-reduce.2
  351.9 700.1 all-reduce.4
  1055.2 27.1 reduce-scatter.1
